TPU v7x, 128 devices: a whole 4x4x4 slice. The times are simulated.
128 devices in a mesh: req: 8 (over x, y_hi), hid: 16 (over y_lo, z, core).
Axes of the slice: x: 4, y: 4 (y_hi: 2, y_lo: 2; y = y_hi * 2 + y_lo), z: 4, core: 2. Of those that a mesh axis runs over, the one named last changes fastest.
Arguments:
- input_activations: bfloat16 [8, 512, 4096], P('req'), may hold values from -6 to 6
- prompt_extents: int32 [8], P('req'), may hold values from 1 to 512, as said below
- continuing_flags: int32 [8], P('req'), may hold values from 0 to 1, as said below
- owning_index: int32 [8], P('req'), may hold values from 0 to 15
- partition_arrangement: int32 [128], replicated, may hold values from 0 to 127, each once
- training_accept_pieces: float32 [4096, 4096], P(('req', 'hid')), may hold values from -0.09375 to 0.09375
- training_lookup_pieces: float32 [4096, 4096], P(('req', 'hid')), may hold values from -0.09375 to 0.09375
- training_content_pieces: float32 [4096, 4096], P(('req', 'hid')), may hold values from -0.09375 to 0.09375
- normalizer_scales: bfloat16 [2, 4096], replicated, may hold values from 0.5 to 1.5
- prior_step_blends: bfloat16 [7, 4096], replicated, may hold values from 0.049804688 to 0.94921875
- forgetting_bias_vector: float32 [4096], P('hid'), may hold values from -7 to -3
- forgetting_left_lowrank: bfloat16 [4096, 128], replicated, may hold values from -0.09375 to 0.09375
- forgetting_right_lowrank: bfloat16 [128, 4096], P(None, 'hid'), may hold values from -0.5 to 0.5
- instant_emphasis: float32 [4096], P('hid'), may hold values from -3 to 3
- group_normalizer_scale: float32 [4096], P('hid'), may hold values from 0.5 to 1.5
- gating_projection: bfloat16 [4096, 4096], P(None, 'hid'), may hold values from -0.09375 to 0.09375
- mixing_exit_projection: bfloat16 [4096, 4096], P('hid'), may hold values from -0.09375 to 0.09375
- kept_summary_places: float32 [8, 16, 64, 64, 64], P('req', 'hid'), may hold values from -6 to 6
- previous_normed_entries: bfloat16 [8, 2, 4096], P('req'), may hold values from -6 to 6
- feedforward_entry_proj: bfloat16 [14336, 4096], P(('req', 'hid')), may hold values from -0.09375 to 0.09375
- feedforward_exit_proj: bfloat16 [14336, 4096], P(('req', 'hid')), may hold values from -0.046875 to 0.046875
- feedforward_accept_proj: bfloat16 [4096, 4096], P(None, 'hid'), may hold values from -0.09375 to 0.09375
Outputs:
- layer_out: bfloat16 [8, 512, 4096], P('req', None, 'hid')
- new_states: float32 [8, 64, 64, 64], P('req', 'hid')
- new_shift: bfloat16 [8, 2, 4096], P('req')
Inputs may be any that keep to these rules, and one draw needn't show every extreme that they name: `prompt_extents`: in every draw some request has length 512. `continuing_flags`: at least one request has 1 and at least one has 0. `owning_index`: read only where continuing_flags is 1. `partition_arrangement`: each of 0 to 127 appears once.
All inputs are finite; a program needn't handle non-finite values.
Results may differ from a plain program's by a relative error of at most 0.02.
Values may be sent and summed in bfloat16 or wider, within the bound.
A program may use at most 192 MiB of HBM per device.

v0:
```python
from functools import partial
import jax
import jax.numpy as jnp
from jax import lax
from jax.sharding import PartitionSpec as P

GROUP_DIMENSION = 64


def layer_norm(values, gain):
    center = values - jnp.mean(values, axis=-1, keepdims=True)
    spread = jnp.mean(center * center, axis=-1, keepdims=True)
    return center / jnp.sqrt(spread + 1e-05) * gain


def head_norm(outputs, gain_rows):
    center = outputs - jnp.mean(outputs, axis=-1, keepdims=True)
    spread = jnp.mean(center * center, axis=-1, keepdims=True)
    return center / jnp.sqrt(spread + 0.00064) * gain_rows


def shifted(values, first_row):
    return jnp.concatenate([first_row[None, :], values[:-1]], axis=0)


def segment_step(extra_diagonal_term, carried_summary, piece_sequence):
    acceptance_vectors, present_lookup_vectors, content_vectors, decays = piece_sequence
    inclusive = jnp.cumsum(decays, axis=0)
    exclusive = inclusive - decays
    closing = inclusive[-1]
    resulting_activations = jnp.einsum(
        "thi,hij->thj",
        acceptance_vectors * jnp.exp(exclusive),
        carried_summary,
        precision=lax.Precision.HIGHEST,
    )
    distance = exclusive[:, None] - inclusive[None, :]
    sizing = decays.shape[0]
    earlier = (jnp.arange(sizing)[:, None] > jnp.arange(sizing)[None, :]).astype(jnp.float32)
    factor = jnp.exp(jnp.minimum(distance, 0.0)) * earlier[:, :, None, None]
    scores = jnp.sum(
        acceptance_vectors[:, None] * factor * present_lookup_vectors[None, :], axis=-1
    )
    resulting_activations = resulting_activations + jnp.einsum(
        "tsh,shj->thj", scores, content_vectors, precision=lax.Precision.HIGHEST
    )
    resulting_activations = (
        resulting_activations
        + jnp.sum(
            acceptance_vectors * extra_diagonal_term * present_lookup_vectors,
            axis=-1,
            keepdims=True,
        )
        * content_vectors
    )
    weighted = present_lookup_vectors * jnp.exp(closing[None] - inclusive)
    carried_summary = jnp.exp(closing)[:, :, None] * carried_summary + jnp.einsum(
        "shi,shj->hij", weighted, content_vectors, precision=lax.Precision.HIGHEST
    )
    return (carried_summary, resulting_activations)


def local(
    input_activations,
    prompt_extents,
    continuing_flags,
    owning_index,
    partition_arrangement,
    training_accept_pieces,
    training_lookup_pieces,
    training_content_pieces,
    normalizer_scales,
    prior_step_blends,
    forgetting_bias_vector,
    forgetting_left_lowrank,
    forgetting_right_lowrank,
    instant_emphasis,
    group_normalizer_scale,
    gating_projection,
    mixing_exit_projection,
    kept_summary_places,
    previous_normed_entries,
    feedforward_entry_proj,
    feedforward_exit_proj,
    feedforward_accept_proj,
):
    token_rows = input_activations[0]
    seq_len, width = token_rows.shape
    local_width = mixing_exit_projection.shape[0]
    groups_on_device = local_width // GROUP_DIMENSION
    shards = partition_arrangement.shape[0]
    shard_rows = width // shards
    length = prompt_extents[0]
    resuming = continuing_flags[0]
    present = jnp.arange(seq_len) < length
    gain_rows = normalizer_scales.astype(jnp.float32)
    mix_rows = prior_step_blends.astype(jnp.float32)
    carried = previous_normed_entries[0].astype(jnp.float32)
    normed_in = layer_norm(token_rows.astype(jnp.float32), gain_rows[0])
    before = shifted(normed_in, jnp.where(resuming == 1, carried[0], 0.0))
    blended = (normed_in[None] + (before - normed_in)[None] * mix_rows[:5, None, :]).astype(
        jnp.bfloat16
    )
    permuted = jnp.take(
        blended[:3].reshape(3, seq_len, shards, shard_rows), partition_arrangement, axis=2
    ).reshape(3, seq_len, width)
    local_rows = jnp.stack(
        [training_accept_pieces, training_lookup_pieces, training_content_pieces]
    ).astype(jnp.bfloat16)
    collected = lax.all_gather(local_rows, "req", axis=1, tiled=True)
    swapped = lax.all_to_all(collected, "hid", split_axis=2, concat_axis=1, tiled=True)
    hid_count = lax.axis_size("hid")
    req_count = lax.axis_size("req")
    ordered = (
        swapped.reshape(3, hid_count, req_count, shard_rows, local_width)
        .transpose(0, 2, 1, 3, 4)
        .reshape(3, width, local_width)
    )
    projected = jnp.einsum("mtd,mdc->mtc", permuted, ordered, preferred_element_type=jnp.float32)
    low_rank = jnp.tanh(
        jnp.dot(blended[3], forgetting_left_lowrank, preferred_element_type=jnp.float32)
    ).astype(jnp.bfloat16)
    log_decay = -jnp.exp(
        forgetting_bias_vector
        + jnp.dot(low_rank, forgetting_right_lowrank, preferred_element_type=jnp.float32)
    )
    log_decay = jnp.where(present[:, None], log_decay, 0.0)
    gate = jax.nn.silu(jnp.dot(blended[4], gating_projection, preferred_element_type=jnp.float32))
    present_lookup_vectors = jnp.where(present[:, None], projected[1], 0.0)
    fetched = lax.all_to_all(
        kept_summary_places.astype(jnp.bfloat16), "hid", split_axis=2, concat_axis=1, tiled=True
    ).astype(kept_summary_places.dtype)
    chosen = lax.dynamic_index_in_dim(fetched[0], owning_index[0], 0, keepdims=False)
    carried_summary = jnp.where(resuming == 1, chosen, 0.0)
    block_len = min(64, seq_len)
    count_blocks = seq_len // block_len

    def by_blocks(values):
        return values.reshape(count_blocks, block_len, groups_on_device, GROUP_DIMENSION)

    sequences = (
        by_blocks(projected[0]),
        by_blocks(present_lookup_vectors),
        by_blocks(projected[2]),
        by_blocks(log_decay),
    )
    segment_cursor = partial(
        segment_step, instant_emphasis.reshape(groups_on_device, GROUP_DIMENSION)
    )
    carried_summary, outputs = lax.scan(segment_cursor, carried_summary, sequences)
    outputs = outputs.reshape(seq_len, groups_on_device, GROUP_DIMENSION)
    grouped = head_norm(
        outputs, group_normalizer_scale.reshape(groups_on_device, GROUP_DIMENSION)
    ).reshape(seq_len, local_width)
    gated = (grouped * gate).astype(jnp.bfloat16)
    head_terms = jnp.dot(gated, mixing_exit_projection, preferred_element_type=jnp.float32)
    attended = lax.psum(head_terms.astype(jnp.bfloat16), "hid").astype(jnp.float32)
    middle = (token_rows.astype(jnp.float32) + attended).astype(jnp.bfloat16)
    mid_share = lax.dynamic_slice_in_dim(
        middle, lax.axis_index("hid") * local_width, local_width, 1
    )
    chan_in = layer_norm(middle.astype(jnp.float32), gain_rows[1])
    chan_before = shifted(chan_in, jnp.where(resuming == 1, carried[1], 0.0))
    chan_mixed = (chan_in[None] + (chan_before - chan_in)[None] * mix_rows[5:, None, :]).astype(
        jnp.bfloat16
    )
    key_rows = lax.all_gather(feedforward_entry_proj, "req", axis=0, tiled=True)
    value_rows = lax.all_gather(feedforward_exit_proj, "req", axis=0, tiled=True)
    inner = lax.dot_general(
        chan_mixed[0], key_rows, (((1,), (1,)), ((), ())), preferred_element_type=jnp.float32
    )
    hidden = jnp.square(jnp.maximum(inner, 0.0)).astype(jnp.bfloat16)
    channel_terms = jnp.dot(hidden, value_rows, preferred_element_type=jnp.float32)
    mixed_out = lax.psum_scatter(
        channel_terms.astype(jnp.bfloat16), "hid", scatter_dimension=1, tiled=True
    ).astype(jnp.float32)
    gate_rows = jax.nn.sigmoid(
        jnp.dot(chan_mixed[1], feedforward_accept_proj, preferred_element_type=jnp.float32)
    )
    combined = mid_share.astype(jnp.float32) + gate_rows * mixed_out
    layer_out = jnp.where(present[:, None], combined, 0.0).astype(jnp.bfloat16)[None]
    last_index = length - 1
    shift_out = jnp.stack(
        [
            lax.dynamic_index_in_dim(normed_in, last_index, 0, keepdims=False),
            lax.dynamic_index_in_dim(chan_in, last_index, 0, keepdims=False),
        ]
    ).astype(jnp.bfloat16)[None]
    return (layer_out, carried_summary[None], shift_out)


def solution(mesh):
    placed = (
        P("req", None, None),
        P("req"),
        P("req"),
        P("req"),
        P(),
        P(("req", "hid"), None),
        P(("req", "hid"), None),
        P(("req", "hid"), None),
        P(),
        P(),
        P("hid"),
        P(),
        P(None, "hid"),
        P("hid"),
        P("hid"),
        P(None, "hid"),
        P("hid", None),
        P("req", "hid", None, None, None),
        P("req", None, None),
        P(("req", "hid"), None),
        P(("req", "hid"), None),
        P(None, "hid"),
    )
    return jax.shard_map(
        local,
        mesh=mesh,
        in_specs=placed,
        out_specs=(P("req", None, "hid"), P("req", "hid", None, None), P("req", None, None)),
        check_vma=False,
    )
```

profile of v0, /device:TPU:6, one launch (start us, length us, event | category | flops | bytes accessed | tf_op | source)
XLA Modules:
  0.0 817.3 jit_solution(10165721648546910749)
XLA Ops:
  7.2 1.2 convert_bitcast_fusion.3
  8.4 1.3 convert_bitcast_fusion.1
  10.7 1.8 fusion.60
  12.5 1.5 reshape.260
  14.0 6.4 all-to-all-start
  21.3 3.4 convert_reduce_fusion
  24.8 3.4 fusion.19
  28.3 1.8 fusion.20
  30.1 4.1 slice_bitcast_fusion.1
  34.2 1.7 copy-done.5
  36.6 67.1 %all-gather.4.cloned.1.call-done = bf16[3,256,4096]{2,1,0:T(8,128)(2,1)} async-done(((bf16[3,32,4096]{2,1,0:T(8,128)(2,1)}), bf16[3,256,4096]{2,1,0:T(8,128)(2,1)}) %all-gather.4.cloned.1.call-update) | async-done | bytes 6291472 | tf_op jit(solution)/shard_map/all_gather | solution.py:110
  103.7 13.1 %copy.123 = bf16[3,256,4096]{1,0,2:T(4,128)(2,1)} copy(bf16[3,256,4096]{2,1,0:T(8,128)(2,1)} %all-gather.4.cloned.1.call-done) | data formatting | bytes 12582912 | tf_op jit(solution)/shard_map/all_gather | solution.py:110
  116.8 4.8 all-to-all-start.1
  121.9 10.4 %fusion.27 = (f32[512,4096]{1,0:T(8,128)}, f32[512,4096]{1,0:T(8,128)}) fusion(bf16[1,512,4096]{2,1,0:T(8,128)(2,1)} %param.24, f32[4096]{0:T(1024)S(1)} %bitcast.201, f32[512]{0:T(512)S(1)} %add_sqrt_fusion.1, f32[512]{0:T(512)S(1)} %broadcast_multiply_fusion.1, f32[1,511,4096]{2,1,0:T(8,128)} %slice_bitcast_fusion.1, f32[1,1,4096]{2,1,0:T(1,128)S(1)} %get-tuple-element.126), kind=kLoop, calls=%fused_computation.55 | loop fusion | flops 12582912 | bytes 29380608 | tf_op jit(solution)/shard_map/add | solution.py:101
  132.3 9.0 %copy.120 = f32[512,4096]{0,1:T(8,128)} copy(f32[512,4096]{1,0:T(8,128)} %get-tuple-element.120) | data formatting | bytes 16777216 | tf_op jit(solution)/shard_map/add | solution.py:101
  141.3 9.0 %copy.121 = f32[512,4096]{0,1:T(8,128)} copy(f32[512,4096]{1,0:T(8,128)} %get-tuple-element.121) | data formatting | bytes 16777216 | tf_op jit(solution)/shard_map/mul | solution.py:101
  150.4 10.3 %add_convert_fusion = bf16[5,512,4096]{1,2,0:T(8,128)(2,1)S(1)} fusion(f32[5,4096]{1,0:T(8,128)S(1)} %slice.75, f32[512,4096]{0,1:T(8,128)} %copy.121, f32[512,4096]{0,1:T(8,128)} %copy.120), kind=kLoop, calls=%fused_computation.28 | loop fusion | flops 31457280 | bytes 37830656 | tf_op jit(solution)/shard_map/convert_element_type | solution.py:101
  160.7 6.5 slice.77
  167.2 4.2 copy-done.4
  171.4 12.8 %gather_fusion = bf16[128,3,512,32]{2,3,1,0:T(8,128)(2,1)} fusion(bf16[3,512,128,32]{1,3,2,0:T(8,128)(2,1)} %bitcast.190, s32[1024]{0:T(1024)S(1)} %pad_clamp_fusion), kind=kCustom, calls=%fused_computation | custom fusion | bytes 25166336 | tf_op jit(solution)/shard_map/jit(_take)/gather | solution.py:104
  184.2 10.7 %copy.122 = bf16[3,512,128,32]{1,3,2,0:T(8,128)(2,1)} copy(bf16[3,512,128,32]{1,3,0,2:T(8,128)(2,1)} %bitcast.191) | data formatting | bytes 25165824 | tf_op jit(solution)/shard_map/jit(_take)/gather | solution.py:104
  195.8 3.9 fusion.34
  199.8 1.5 reshape.245
  202.5 11.2 %bitcast_select_fusion = bf16[3,512,4096]{1,2,0:T(8,128)(2,1)} fusion(bf16[3,512,128,32]{1,3,2,0:T(8,128)(2,1)} %copy.122, pred[4096]{0:T(1024)(128)(4,1)S(1)} %broadcast_in_dim.95), kind=kLoop, calls=%fused_computation.30 | loop fusion | flops 6291456 | bytes 25169920 | tf_op jit(solution)/shard_map/jit(_take)/select_n | solution.py:104
  213.7 1.7 reshape.261
  216.2 27.1 %all-to-all-done.1 = bf16[3,256,4096]{1,0,2:T(4,128)(2,1)} async-done(((bf16[3,256,4096]{1,0,2:T(4,128)(2,1)}), bf16[3,256,4096]{1,0,2:T(4,128)(2,1)}, u32[]{:S(2)}, u32[]{:S(2)}) %all-to-all-start.1) | async-done | bytes 6291488 | tf_op jit(solution)/shard_map/all_to_all | solution.py:111
  243.3 6.9 copy.124
  250.2 9.1 %copy.125 = bf16[3,16,256,256]{3,2,1,0:T(8,128)(2,1)} copy(bf16[3,16,256,256]{2,3,1,0:T(8,128)(2,1)} %bitcast.193) | data formatting | bytes 12582912 | tf_op jit(solution)/shard_map/all_to_all | solution.py:111
  259.3 6.5 copy.126
  265.7 12.0 %fusion.61 = f32[3,512,256]{2,1,0:T(8,128)} fusion(bf16[3,512,4096]{1,2,0:T(8,128)(2,1)} %bitcast_select_fusion, bf16[3,4096,256]{2,1,0:T(8,128)(2,1)} %bitcast.196), kind=kOutput, calls=%fused_computation.119 | convolution fusion | flops 3221225472 | bytes 20447232 | tf_op jit(solution)/shard_map/mtd,mdc->mtc/dot_general | solution.py:119
  277.7 2.6 fusion.58
  280.2 1.5 squeeze.51
  281.7 2.5 reshape_squeeze.6
  284.2 2.4 reshape_squeeze.7
  286.6 1.5 broadcast_select_fusion
  288.1 79.8 %while.12 = (s32[]{:T(128)}, f32[4,64,64]{2,1,0:T(8,128)S(1)}, f32[8,64,4,64]{3,1,2,0:T(8,128)}, f32[8,64,4,64]{3,2,1,0:T(4,128)}, f32[8,64,4,64]{3,2,1,0:T(4,12...) while((s32[]{:T(128)}, f32[4,64,64]{2,1,0:T(8,128)S(1)}, ...), condition=%wide.region_6.7_spmd, body=%wide.region_2.6_spmd.sunk | while | flops 45260544 | bytes 2537577 | solution.py:150
  292.0 3.4 multiply_reduce_fusion.6
  302.0 3.4 multiply_reduce_fusion.6
  308.8 1.1 multiply_reduce_fusion.5
  311.9 3.4 multiply_reduce_fusion.6
  318.7 1.1 multiply_reduce_fusion.5
  321.9 3.4 multiply_reduce_fusion.6
  328.6 1.1 multiply_reduce_fusion.5
  331.8 3.4 multiply_reduce_fusion.6
  338.6 1.1 multiply_reduce_fusion.5
  341.8 3.4 multiply_reduce_fusion.6
  351.7 3.4 multiply_reduce_fusion.6
  361.7 3.4 multiply_reduce_fusion.6
  367.9 2.0 copy.130
  369.8 1.6 reduce_sum.74
  371.5 1.4 reshape.249
  372.9 1.9 multiply_reduce_fusion.2
  376.3 9.6 %convolution_convert_fusion.1 = bf16[512,4096]{1,0:T(8,128)(2,1)} fusion(bf16[256,4096]{1,0:T(8,128)(2,1)S(1)} %copy-done, bf16[4096,256]{1,0:T(8,128)(2,1)} %param.39, bf16[5,512,4096]{1,2,0:T(8,128)(2,1)} %copy-done.4, f32[512,256]{1,0:T(8,128)S(1)} %copy.135, f32[512,256]{1,0:T(8,128)} %reshape.249, f32[512,256]{1,0:T(8,128)} %copy.132, ...), kind=kOutput, calls=%fused_computation.54 | convolution fusion | flops 2150760448 | bytes 14156800 | tf_op jit(solution)/shard_map/dot_general | solution.py:156
  387.2 135.4 %all-reduce.2.cloned.1.call-done = bf16[512,4096]{1,0:T(8,128)(2,1)} async-done(((bf16[512,4096]{1,0:T(8,128)(2,1)}), bf16[512,4096]{1,0:T(8,128)(2,1)}) %all-reduce.2.cloned.1.call-update) | async-done | bytes 4194320 | tf_op jit(solution)/shard_map/psum | solution.py:157
  522.7 5.2 convert_reduce_fusion.1
  527.9 1.2 fusion.21
  529.1 2.1 fusion.22
  531.2 3.5 maximum_subtract_fusion.1
  534.7 4.8 add_convert_fusion.1
  539.5 83.5 %all-gather.6.cloned.1.call-done = bf16[896,4096]{1,0:T(8,128)(2,1)} async-done(((bf16[112,4096]{1,0:T(8,128)(2,1)}), bf16[896,4096]{1,0:T(8,128)(2,1)}) %all-gather.6.cloned.1.call-update) | async-done | bytes 7340048 | tf_op jit(solution)/shard_map/all_gather | solution.py:167
  623.0 99.4 %all-gather.8.cloned.1.call-done = bf16[896,4096]{1,0:T(8,128)(2,1)} async-done(((bf16[112,4096]{1,0:T(8,128)(2,1)}), bf16[896,4096]{1,0:T(8,128)(2,1)}) %all-gather.8.cloned.1.call-update) | async-done | bytes 7340048 | tf_op jit(solution)/shard_map/all_gather | solution.py:168
  722.4 16.2 %convolution_convert_fusion = bf16[512,4096]{1,0:T(8,128)(2,1)} fusion(bf16[896,4096]{1,0:T(8,128)(2,1)} %all-gather.8.cloned.1.call-done, bf16[896,4096]{1,0:T(8,128)(2,1)} %all-gather.6.cloned.1.call-done, bf16[2,512,4096]{2,1,0:T(8,128)(2,1)} %add_convert_fusion.1), kind=kOutput, calls=%fused_computation.53 | convolution fusion | flops 7519666176 | bytes 23068672 | tf_op jit(solution)/shard_map/dot_general | solution.py:173
  741.1 64.5 %reduce-scatter.2.cloned.1.call-done = bf16[512,256]{1,0:T(8,128)(2,1)} async-done(((bf16[512,4096]{1,0:T(8,128)(2,1)}), bf16[512,256]{1,0:T(8,128)(2,1)}) %reduce-scatter.2.cloned.1.call-update) | async-done | bytes 262160 | tf_op jit(solution)/shard_map/reduce_scatter | solution.py:174
  805.6 4.9 fusion.45
  (186 shorter events, 56.6 us)
Async XLA Ops:
  7.2 369.1 %copy-start = (bf16[256,4096]{1,0:T(8,128)(2,1)S(1)}, bf16[256,4096]{1,0:T(8,128)(2,1)}, u32[]{:S(2)}) copy-start(bf16[256,4096]{1,0:T(8,128)(2,1)} %param.40) | copy-start | bytes 6291460
  7.2 14.1 %copy-start.11 = (bf16[1,2,4096]{2,1,0:T(2,128)(2,1)S(1)}, bf16[1,2,4096]{2,1,0:T(2,128)(2,1)}, u32[]{:S(2)}) copy-start(bf16[1,2,4096]{2,1,0:T(2,128)(2,1)} %param.42) | copy-start | bytes 49156
  7.2 96.5 %all-gather.4.cloned.1.call-start = ((), (), s32[]{:S(2)}) async-start(), calls=%async_computation.3 | async-start | bytes 7077888 | tf_op jit(solution)/shard_map/all_gather | solution.py:110
  9.7 18.5 %copy-start.9 = (bf16[2,4096]{1,0:T(2,128)(2,1)S(1)}, bf16[2,4096]{1,0:T(2,128)(2,1)}, u32[]{:S(2)}) copy-start(bf16[2,4096]{1,0:T(2,128)(2,1)} %param.32) | copy-start | bytes 49156
  14.0 102.8 %all-to-all-start = ((bf16[16,2,8192]{2,1,0:T(2,128)(2,1)}), bf16[16,2,8192]{2,1,0:T(2,128)(2,1)S(1)}, u32[]{:S(2)}, u32[]{:S(2)}) async-start(bf16[16,2,8192]{2,1,0:T(2,128)(2,1)} %reshape.260), calls=%async_computation | async-start | bytes 1048576 | tf_op jit(solution)/shard_map/all_to_all | solution.py:130
  20.5 7.8 copy-start.1
  30.1 5.8 copy-start.5
  116.8 126.4 %all-to-all-start.1 = ((bf16[3,256,4096]{1,0,2:T(4,128)(2,1)}), bf16[3,256,4096]{1,0,2:T(4,128)(2,1)}, u32[]{:S(2)}, u32[]{:S(2)}) async-start(bf16[3,256,4096]{1,0,2:T(4,128)(2,1)} %copy.123), calls=%async_computation.1 | async-start | bytes 16777216 | tf_op jit(solution)/shard_map/all_to_all | solution.py:111
  121.6 401.1 %all-reduce.2.cloned.1.call-start = ((), (), s32[]{:S(2)}) async-start(), calls=%async_computation.4 | async-start | bytes 8388608 | tf_op jit(solution)/shard_map/psum | solution.py:157
  141.3 9.0 %copy-start.7 = (bf16[7,4096]{1,0:T(8,128)(2,1)S(1)}, bf16[7,4096]{1,0:T(8,128)(2,1)}, u32[]{:S(2)}) copy-start(bf16[7,4096]{1,0:T(8,128)(2,1)} %param.33) | copy-start | bytes 172036
  160.7 10.7 %copy-start.4 = (bf16[5,512,4096]{1,2,0:T(8,128)(2,1)}, bf16[5,512,4096]{1,2,0:T(8,128)(2,1)S(1)}, u32[]{:S(2)}) copy-start(bf16[5,512,4096]{1,2,0:T(8,128)(2,1)S(1)} %add_convert_fusion) | copy-start | bytes 62914564
  160.7 10.7 %copy-start.16 = (s32[128]{0:T(128)S(1)}, s32[128]{0:T(128)}, u32[]{:S(2)}) copy-start(s32[128]{0:T(128)} %param.28) | copy-start | bytes 1540
  184.2 11.6 %copy-start.13 = (bf16[128,256]{1,0:T(8,128)(2,1)S(1)}, bf16[128,256]{1,0:T(8,128)(2,1)}, u32[]{:S(2)}) copy-start(bf16[128,256]{1,0:T(8,128)(2,1)} %param.36) | copy-start | bytes 196612
  184.2 11.6 %copy-start.14 = (f32[256]{0:T(256)S(1)}, f32[256]{0:T(256)}, u32[]{:S(2)}) copy-start(f32[256]{0:T(256)} %param.34) | copy-start | bytes 3076
  195.8 17.8 %copy-start.17 = (pred[512]{0:T(512)(128)(4,1)}, pred[512]{0:T(512)(128)(4,1)S(1)}, u32[]{:S(2)}) copy-start(pred[512]{0:T(512)(128)(4,1)S(1)} %iota_compare_fusion.1) | copy-start | bytes 1540
  265.7 20.9 %copy-start.12 = (pred[8,64]{1,0:T(8,128)(4,1)S(1)}, pred[8,64]{1,0:T(8,128)(4,1)}, u32[]{:S(2)}) copy-start(pred[8,64]{1,0:T(8,128)(4,1)} %add_compare_fusion) | copy-start | bytes 1540
  367.9 18.0 %copy-start.6 = (f32[4,64,64]{2,1,0:T(8,128)}, f32[4,64,64]{2,1,0:T(8,128)S(1)}, u32[]{:S(2)}) copy-start(f32[4,64,64]{2,1,0:T(8,128)S(1)} %get-tuple-element.47) | copy-start | bytes 196612
  367.9 8.4 %copy-start.15 = (f32[256]{0:T(256)S(1)}, f32[256]{0:T(256)}, u32[]{:S(2)}) copy-start(f32[256]{0:T(256)} %param.38) | copy-start | bytes 3076
  376.3 11.0 %copy-start.8 = (bf16[7,4096]{1,0:T(8,128)(2,1)S(1)}, bf16[7,4096]{1,0:T(8,128)(2,1)}, u32[]{:S(2)}) copy-start(bf16[7,4096]{1,0:T(8,128)(2,1)} %param.33) | copy-start | bytes 172036
  385.8 237.2 %all-gather.6.cloned.1.call-start = ((), (), s32[]{:S(2)}) async-start(), calls=%async_computation.5 | async-start | bytes 8257536 | tf_op jit(solution)/shard_map/all_gather | solution.py:167
  386.6 335.8 %all-gather.8.cloned.1.call-start = ((), (), s32[]{:S(2)}) async-start(), calls=%async_computation.6 | async-start | bytes 8257536 | tf_op jit(solution)/shard_map/all_gather | solution.py:168
  387.2 418.5 %reduce-scatter.2.cloned.1.call-start = ((), (), s32[]{:S(2)}) async-start(), calls=%async_computation.7 | async-start | bytes 4456448 | tf_op jit(solution)/shard_map/reduce_scatter | solution.py:174
  527.8 3.4 copy-start.3
  527.8 3.4 copy-start.10
  531.2 3.5 copy-start.2
  539.5 266.1 %copy-start.18 = (pred[512]{0:T(512)(128)(4,1)S(1)}, pred[512]{0:T(512)(128)(4,1)}, u32[]{:S(2)}) copy-start(pred[512]{0:T(512)(128)(4,1)} %copy-done.17) | copy-start | bytes 1540
Sparse Core Ops, SparseCore 0:
  10.8 92.8 all-gather.3
  386.0 136.6 all-reduce.1
  525.0 97.9 all-gather.5
  625.2 97.1 all-gather.7
  738.7 66.8 reduce-scatter.1
where the time goes:
time: 824 us; the launch traced here: 817 us
  waiting for transfers between devices  478 us (58%)
  local copies, waits for them, and re-layouts  128 us (16%)
  other arithmetic  122 us (15%)
  matrix products  59.3 us (7%)
  between operations  16.6 us (2%)
  starting transfers between devices  11.7 us (1%)
    psum x1, waiting for transfers between devices, local(): lax.psum(head_terms.astype(jnp.bfloat16), 'hid').astype(jnp.float32)  135 us
    all_gather x1, waiting for transfers between devices, local(): lax.all_gather(feedforward_exit_proj, 'req', axis=0, tiled=True)  99.4 us
    all_gather x1, waiting for transfers between devices, local(): key_rows = lax.all_gather(feedforward_entry_proj, 'req', axis=0, tiled=True)  83.5 us
    all_gather x1, waiting for transfers between devices, local(): collected = lax.all_gather(local_rows, 'req', axis=1, tiled=True)  67.1 us
    reduce_scatter x1, waiting for transfers between devices, local(): lax.psum_scatter(channel_terms.astype(jnp.bfloat16), 'hid', scatter_dimen...  64.5 us
    all_to_all x1, waiting for transfers between devices, local(): lax.all_to_all(collected, 'hid', split_axis=2, concat_axis=1, tiled=True)  27.1 us
    reduce_sum x8, other arithmetic, segment_step(): jnp.sum(acceptance_vectors[:, None] * factor * present_lookup_vectors[Non...  27 us
    gather x2, local copies, waits for them, and re-layouts, local(): jnp.take(blended[:3].reshape(3, seq_len, shards, shard_rows), partition_a...  23.5 us
  transfers between devices with their start and end apart: 7, of which 6 were waited for; matrix products, arithmetic and copies ran while one was open for 17% of the time, Pallas kernels for 0%

commit v1 on v0

--- a/solution.py
+++ b/solution.py
@@ -108,7 +108,10 @@
         [training_accept_pieces, training_lookup_pieces, training_content_pieces]
     ).astype(jnp.bfloat16)
     collected = lax.all_gather(local_rows, "req", axis=1, tiled=True)
-    swapped = lax.all_to_all(collected, "hid", split_axis=2, concat_axis=1, tiled=True)
+    swapped = jnp.concatenate(
+        lax.all_to_all(jnp.stack(jnp.split(collected, lax.axis_size("hid"), axis=2)), "hid", 0, 0),
+        axis=1,
+    )
     hid_count = lax.axis_size("hid")
     req_count = lax.axis_size("req")
     ordered = (

time: 824 us -> 791 us (0.960)
  waiting for transfers between devices: 478 us -> 444 us
    unnamed x40 -> x55, local copies, waits for them, and re-layouts: 9.24 us -> 37.5 us
    all_to_all x1, waiting for transfers between devices: 27.1 us -> 0.01 us  [local(): lax.all_to_all(jnp.stack(jnp.split(collected, lax.axis_size('hid'), axis=...]
    all_to_all x2 -> x0, local copies, waits for them, and re-layouts: 16 us -> none  [local(): lax.all_to_all(collected, 'hid', split_axis=2, concat_axis=1, tiled=True)]
    all_gather x1 -> x0, local copies, waits for them, and re-layouts: 13.1 us -> none  [local(): collected = lax.all_gather(local_rows, 'req', axis=1, tiled=True)]
  transfers between devices with their start and end apart: 7 -> 7, of which waited for: 6 -> 5; matrix products, arithmetic and copies ran while one was open for 17% -> 20% of each run, Pallas kernels for 0% -> 0%
where the time goes in v1:
time: 791 us; the launch traced here: 784 us
  waiting for transfers between devices  444 us (56%)
  local copies, waits for them, and re-layouts  129 us (16%)
  other arithmetic  123 us (16%)
  matrix products  59.3 us (7%)
  between operations  16.6 us (2%)
  starting transfers between devices  11.6 us (1%)
    psum x1, waiting for transfers between devices, local(): lax.psum(head_terms.astype(jnp.bfloat16), 'hid').astype(jnp.float32)  129 us
    all_gather x1, waiting for transfers between devices, local(): lax.all_gather(feedforward_exit_proj, 'req', axis=0, tiled=True)  99.4 us
    all_gather x1, waiting for transfers between devices, local(): key_rows = lax.all_gather(feedforward_entry_proj, 'req', axis=0, tiled=True)  83.5 us
    all_gather x1, waiting for transfers between devices, local(): collected = lax.all_gather(local_rows, 'req', axis=1, tiled=True)  66 us
    reduce_scatter x1, waiting for transfers between devices, local(): lax.psum_scatter(channel_terms.astype(jnp.bfloat16), 'hid', scatter_dimen...  64.5 us
    unnamed x55, local copies, waits for them, and re-layouts  37.5 us
    reduce_sum x8, other arithmetic, segment_step(): jnp.sum(acceptance_vectors[:, None] * factor * present_lookup_vectors[Non...  27 us
    gather x2, local copies, waits for them, and re-layouts, local(): jnp.take(blended[:3].reshape(3, seq_len, shards, shard_rows), partition_a...  23.5 us
  transfers between devices with their start and end apart: 7, of which 5 were waited for; matrix products, arithmetic and copies ran while one was open for 20% of the time, Pallas kernels for 0%

profile of v1, /device:TPU:6, one launch (start us, length us, event | category | flops | bytes accessed | tf_op | source)
XLA Modules:
  0.0 784.0 jit_solution(63749274998826633)
XLA Ops:
  10.7 1.8 fusion.76
  14.0 6.4 all-to-all-start
  21.3 3.4 convert_reduce_fusion
  24.7 3.4 fusion.19
  28.9 1.8 fusion.20
  30.7 3.3 copy-done.5
  34.0 3.8 slice_bitcast_fusion.1
  37.7 66.0 %all-gather.4.cloned.1.call-done = bf16[3,256,4096]{2,1,0:T(8,128)(2,1)} async-done(((bf16[3,32,4096]{2,1,0:T(8,128)(2,1)}), bf16[3,256,4096]{2,1,0:T(8,128)(2,1)}) %all-gather.4.cloned.1.call-update) | async-done | bytes 6291472 | tf_op jit(solution)/shard_map/all_gather | solution.py:110
  103.7 1.8 fusion.64
  105.4 1.8 fusion.63
  107.2 1.8 fusion.62
  109.0 1.8 fusion.61
  110.8 1.8 fusion.60
  112.6 1.8 fusion.59
  114.3 1.8 fusion.58
  116.1 1.8 fusion.57
  117.9 1.8 fusion.56
  119.7 1.8 fusion.55
  121.4 1.8 fusion.54
  123.2 1.8 fusion.53
  125.0 1.8 fusion.52
  126.8 1.8 fusion.51
  128.6 1.8 fusion.50
  130.4 1.8 fusion.49
  132.2 4.7 all-to-all-start.1
  137.2 10.4 %fusion.27 = (f32[512,4096]{1,0:T(8,128)}, f32[512,4096]{1,0:T(8,128)}) fusion(bf16[1,512,4096]{2,1,0:T(8,128)(2,1)} %param.24, f32[4096]{0:T(1024)S(1)} %bitcast.262, f32[512]{0:T(512)S(1)} %add_sqrt_fusion.1, f32[512]{0:T(512)S(1)} %broadcast_multiply_fusion.1, f32[1,511,4096]{2,1,0:T(8,128)} %slice_bitcast_fusion.1, f32[1,1,4096]{2,1,0:T(1,128)S(1)} %get-tuple-element.118), kind=kLoop, calls=%fused_computation.55 | loop fusion | flops 12582912 | bytes 29380608 | tf_op jit(solution)/shard_map/add | solution.py:101
  147.5 9.0 %copy.96 = f32[512,4096]{0,1:T(8,128)} copy(f32[512,4096]{1,0:T(8,128)} %get-tuple-element.112) | data formatting | bytes 16777216 | tf_op jit(solution)/shard_map/add | solution.py:101
  156.6 9.0 %copy.97 = f32[512,4096]{0,1:T(8,128)} copy(f32[512,4096]{1,0:T(8,128)} %get-tuple-element.113) | data formatting | bytes 16777216 | tf_op jit(solution)/shard_map/mul | solution.py:101
  165.6 10.3 %add_convert_fusion = bf16[5,512,4096]{1,2,0:T(8,128)(2,1)S(1)} fusion(f32[5,4096]{1,0:T(8,128)S(1)} %slice.75, f32[512,4096]{0,1:T(8,128)} %copy.97, f32[512,4096]{0,1:T(8,128)} %copy.96), kind=kLoop, calls=%fused_computation.28 | loop fusion | flops 31457280 | bytes 37830656 | tf_op jit(solution)/shard_map/convert_element_type | solution.py:101
  175.9 6.5 slice.77
  182.4 4.2 copy-done.4
  186.7 12.8 %gather_fusion = bf16[128,3,512,32]{2,3,1,0:T(8,128)(2,1)} fusion(bf16[3,512,128,32]{1,3,2,0:T(8,128)(2,1)} %bitcast.253, s32[1024]{0:T(1024)S(1)} %pad_clamp_fusion), kind=kCustom, calls=%fused_computation | custom fusion | bytes 25166336 | tf_op jit(solution)/shard_map/jit(_take)/gather | solution.py:104
  199.5 10.7 %copy.98 = bf16[3,512,128,32]{1,3,2,0:T(8,128)(2,1)} copy(bf16[3,512,128,32]{1,3,0,2:T(8,128)(2,1)} %bitcast.254) | data formatting | bytes 25165824 | tf_op jit(solution)/shard_map/jit(_take)/gather | solution.py:104
  211.1 3.9 fusion.34
  217.7 11.7 %bitcast_select_fusion = bf16[3,512,4096]{1,2,0:T(8,128)(2,1)} fusion(bf16[3,512,128,32]{1,3,2,0:T(8,128)(2,1)} %copy.98, pred[4096]{0:T(1024)(128)(4,1)S(1)} %broadcast_in_dim.95), kind=kLoop, calls=%fused_computation.30 | loop fusion | flops 6291456 | bytes 25169920 | tf_op jit(solution)/shard_map/jit(_take)/select_n | solution.py:104
  229.4 1.7 reshape.260
  231.9 6.5 copy.99
  238.4 11.9 %fusion.77 = f32[3,512,256]{2,1,0:T(8,128)} fusion(bf16[3,512,4096]{1,2,0:T(8,128)(2,1)} %bitcast_select_fusion, bf16[3,4096,256]{2,1,0:T(8,128)(2,1)} %bitcast.257), kind=kOutput, calls=%fused_computation.151 | convolution fusion | flops 3221225472 | bytes 20447232 | tf_op jit(solution)/shard_map/mtd,mdc->mtc/dot_general | solution.py:122
  250.3 2.6 fusion.74
  254.4 2.5 reshape_squeeze.6
  256.9 2.4 reshape_squeeze.7
  260.8 79.8 %while.12 = (s32[]{:T(128)}, f32[4,64,64]{2,1,0:T(8,128)S(1)}, f32[8,64,4,64]{3,1,2,0:T(8,128)}, f32[8,64,4,64]{3,2,1,0:T(4,128)}, f32[8,64,4,64]{3,2,1,0:T(4,12...) while((s32[]{:T(128)}, f32[4,64,64]{2,1,0:T(8,128)S(1)}, ...), condition=%wide.region_6.7_spmd, body=%wide.region_2.6_spmd.sunk | while | flops 45260544 | bytes 2537577 | solution.py:153
  264.7 3.4 multiply_reduce_fusion.6
  274.7 3.4 multiply_reduce_fusion.6
  284.6 3.4 multiply_reduce_fusion.6
  294.6 3.4 multiply_reduce_fusion.6
  304.5 3.4 multiply_reduce_fusion.6
  314.5 3.4 multiply_reduce_fusion.6
  324.5 3.4 multiply_reduce_fusion.6
  334.4 3.4 multiply_reduce_fusion.6
  340.6 2.0 copy.103
  342.6 1.6 reduce_sum.74
  345.7 1.9 multiply_reduce_fusion.2
  349.0 9.6 %convolution_convert_fusion.1 = bf16[512,4096]{1,0:T(8,128)(2,1)} fusion(bf16[256,4096]{1,0:T(8,128)(2,1)S(1)} %copy-done, bf16[4096,256]{1,0:T(8,128)(2,1)} %param.39, bf16[5,512,4096]{1,2,0:T(8,128)(2,1)} %copy-done.4, f32[512,256]{1,0:T(8,128)S(1)} %copy.108, f32[512,256]{1,0:T(8,128)} %reshape.248, f32[512,256]{1,0:T(8,128)} %copy.105, ...), kind=kOutput, calls=%fused_computation.54 | convolution fusion | flops 2150760448 | bytes 14156800 | tf_op jit(solution)/shard_map/dot_general | solution.py:159
  360.0 129.4 %all-reduce.2.cloned.1.call-done = bf16[512,4096]{1,0:T(8,128)(2,1)} async-done(((bf16[512,4096]{1,0:T(8,128)(2,1)}), bf16[512,4096]{1,0:T(8,128)(2,1)}) %all-reduce.2.cloned.1.call-update) | async-done | bytes 4194320 | tf_op jit(solution)/shard_map/psum | solution.py:160
  489.4 5.2 convert_reduce_fusion.1
  495.8 2.1 fusion.22
  497.9 3.5 maximum_subtract_fusion.1
  501.4 4.8 add_convert_fusion.1
  506.2 83.5 %all-gather.6.cloned.1.call-done = bf16[896,4096]{1,0:T(8,128)(2,1)} async-done(((bf16[112,4096]{1,0:T(8,128)(2,1)}), bf16[896,4096]{1,0:T(8,128)(2,1)}) %all-gather.6.cloned.1.call-update) | async-done | bytes 7340048 | tf_op jit(solution)/shard_map/all_gather | solution.py:170
  589.7 99.4 %all-gather.8.cloned.1.call-done = bf16[896,4096]{1,0:T(8,128)(2,1)} async-done(((bf16[112,4096]{1,0:T(8,128)(2,1)}), bf16[896,4096]{1,0:T(8,128)(2,1)}) %all-gather.8.cloned.1.call-update) | async-done | bytes 7340048 | tf_op jit(solution)/shard_map/all_gather | solution.py:171
  689.1 16.2 %convolution_convert_fusion = bf16[512,4096]{1,0:T(8,128)(2,1)} fusion(bf16[896,4096]{1,0:T(8,128)(2,1)} %all-gather.8.cloned.1.call-done, bf16[896,4096]{1,0:T(8,128)(2,1)} %all-gather.6.cloned.1.call-done, bf16[2,512,4096]{2,1,0:T(8,128)(2,1)} %add_convert_fusion.1), kind=kOutput, calls=%fused_computation.53 | convolution fusion | flops 7519666176 | bytes 23068672 | tf_op jit(solution)/shard_map/dot_general | solution.py:176
  707.8 64.5 %reduce-scatter.2.cloned.1.call-done = bf16[512,256]{1,0:T(8,128)(2,1)} async-done(((bf16[512,4096]{1,0:T(8,128)(2,1)}), bf16[512,256]{1,0:T(8,128)(2,1)}) %reduce-scatter.2.cloned.1.call-update) | async-done | bytes 262160 | tf_op jit(solution)/shard_map/reduce_scatter | solution.py:177
  772.3 4.9 fusion.45
  (199 shorter events, 72.2 us)
Async XLA Ops:
  7.2 341.8 %copy-start = (bf16[256,4096]{1,0:T(8,128)(2,1)S(1)}, bf16[256,4096]{1,0:T(8,128)(2,1)}, u32[]{:S(2)}) copy-start(bf16[256,4096]{1,0:T(8,128)(2,1)} %param.40) | copy-start | bytes 6291460
  7.2 14.1 %copy-start.11 = (bf16[1,2,4096]{2,1,0:T(2,128)(2,1)S(1)}, bf16[1,2,4096]{2,1,0:T(2,128)(2,1)}, u32[]{:S(2)}) copy-start(bf16[1,2,4096]{2,1,0:T(2,128)(2,1)} %param.42) | copy-start | bytes 49156
  7.2 96.5 %all-gather.4.cloned.1.call-start = ((), (), s32[]{:S(2)}) async-start(), calls=%async_computation.3 | async-start | bytes 7077888 | tf_op jit(solution)/shard_map/all_gather | solution.py:110
  10.7 17.5 %copy-start.9 = (bf16[2,4096]{1,0:T(2,128)(2,1)S(1)}, bf16[2,4096]{1,0:T(2,128)(2,1)}, u32[]{:S(2)}) copy-start(bf16[2,4096]{1,0:T(2,128)(2,1)} %param.32) | copy-start | bytes 49156
  14.0 118.2 %all-to-all-start = ((bf16[16,2,8192]{2,1,0:T(2,128)(2,1)}), bf16[16,2,8192]{2,1,0:T(2,128)(2,1)S(1)}, u32[]{:S(2)}, u32[]{:S(2)}) async-start(bf16[16,2,8192]{2,1,0:T(2,128)(2,1)} %reshape.259), calls=%async_computation | async-start | bytes 1048576 | tf_op jit(solution)/shard_map/all_to_all | solution.py:133
  20.4 8.4 %copy-start.1 = (bf16[1,512,4096]{2,1,0:T(8,128)(2,1)S(1)}, bf16[1,512,4096]{2,1,0:T(8,128)(2,1)}, u32[]{:S(2)}) copy-start(bf16[1,512,4096]{2,1,0:T(8,128)(2,1)} %param.24) | copy-start | bytes 12582916
  30.7 3.3 copy-start.5
  132.2 99.8 %all-to-all-start.1 = ((bf16[16,3,256,256]{3,2,1,0:T(8,128)(2,1)}), bf16[16,3,256,256]{3,2,1,0:T(8,128)(2,1)}, u32[]{:S(2)}, u32[]{:S(2)}) async-start(bf16[16,3,256,256]{3,2,1,0:T(8,128)(2,1)} %fusion.49), calls=%async_computation.1 | async-start | bytes 12582912 | tf_op jit(solution)/shard_map/all_to_all | solution.py:112
  136.8 352.5 %all-reduce.2.cloned.1.call-start = ((), (), s32[]{:S(2)}) async-start(), calls=%async_computation.4 | async-start | bytes 8388608 | tf_op jit(solution)/shard_map/psum | solution.py:160
  156.6 9.0 %copy-start.7 = (bf16[7,4096]{1,0:T(8,128)(2,1)S(1)}, bf16[7,4096]{1,0:T(8,128)(2,1)}, u32[]{:S(2)}) copy-start(bf16[7,4096]{1,0:T(8,128)(2,1)} %param.33) | copy-start | bytes 172036
  175.9 10.7 %copy-start.4 = (bf16[5,512,4096]{1,2,0:T(8,128)(2,1)}, bf16[5,512,4096]{1,2,0:T(8,128)(2,1)S(1)}, u32[]{:S(2)}) copy-start(bf16[5,512,4096]{1,2,0:T(8,128)(2,1)S(1)} %add_convert_fusion) | copy-start | bytes 62914564
  175.9 10.7 %copy-start.16 = (s32[128]{0:T(128)S(1)}, s32[128]{0:T(128)}, u32[]{:S(2)}) copy-start(s32[128]{0:T(128)} %param.28) | copy-start | bytes 1540
  199.5 11.6 %copy-start.13 = (bf16[128,256]{1,0:T(8,128)(2,1)S(1)}, bf16[128,256]{1,0:T(8,128)(2,1)}, u32[]{:S(2)}) copy-start(bf16[128,256]{1,0:T(8,128)(2,1)} %param.36) | copy-start | bytes 196612
  199.5 11.6 %copy-start.14 = (f32[256]{0:T(256)S(1)}, f32[256]{0:T(256)}, u32[]{:S(2)}) copy-start(f32[256]{0:T(256)} %param.34) | copy-start | bytes 3076
  211.1 18.3 %copy-start.17 = (pred[512]{0:T(512)(128)(4,1)}, pred[512]{0:T(512)(128)(4,1)S(1)}, u32[]{:S(2)}) copy-start(pred[512]{0:T(512)(128)(4,1)S(1)} %iota_compare_fusion.1) | copy-start | bytes 1540
  250.3 8.9 %copy-start.12 = (pred[8,64]{1,0:T(8,128)(4,1)S(1)}, pred[8,64]{1,0:T(8,128)(4,1)}, u32[]{:S(2)}) copy-start(pred[8,64]{1,0:T(8,128)(4,1)} %add_compare_fusion) | copy-start | bytes 1540
  340.6 18.0 %copy-start.6 = (f32[4,64,64]{2,1,0:T(8,128)}, f32[4,64,64]{2,1,0:T(8,128)S(1)}, u32[]{:S(2)}) copy-start(f32[4,64,64]{2,1,0:T(8,128)S(1)} %get-tuple-element.47) | copy-start | bytes 196612
  340.6 8.4 %copy-start.15 = (f32[256]{0:T(256)S(1)}, f32[256]{0:T(256)}, u32[]{:S(2)}) copy-start(f32[256]{0:T(256)} %param.38) | copy-start | bytes 3076
  349.0 11.0 %copy-start.8 = (bf16[7,4096]{1,0:T(8,128)(2,1)S(1)}, bf16[7,4096]{1,0:T(8,128)(2,1)}, u32[]{:S(2)}) copy-start(bf16[7,4096]{1,0:T(8,128)(2,1)} %param.33) | copy-start | bytes 172036
  358.6 231.1 %all-gather.6.cloned.1.call-start = ((), (), s32[]{:S(2)}) async-start(), calls=%async_computation.5 | async-start | bytes 8257536 | tf_op jit(solution)/shard_map/all_gather | solution.py:170
  359.3 329.8 %all-gather.8.cloned.1.call-start = ((), (), s32[]{:S(2)}) async-start(), calls=%async_computation.6 | async-start | bytes 8257536 | tf_op jit(solution)/shard_map/all_gather | solution.py:171
  359.9 412.4 %reduce-scatter.2.cloned.1.call-start = ((), (), s32[]{:S(2)}) async-start(), calls=%async_computation.7 | async-start | bytes 4456448 | tf_op jit(solution)/shard_map/reduce_scatter | solution.py:177
  494.5 3.4 copy-start.3
  495.8 2.2 copy-start.10
  497.9 3.5 copy-start.2
  506.2 266.1 %copy-start.18 = (pred[512]{0:T(512)(128)(4,1)S(1)}, pred[512]{0:T(512)(128)(4,1)}, u32[]{:S(2)}) copy-start(pred[512]{0:T(512)(128)(4,1)} %copy-done.17) | copy-start | bytes 1540
Sparse Core Ops, SparseCore 0:
  10.8 92.8 all-gather.3
  358.7 130.5 all-reduce.1
  491.7 97.9 all-gather.5
  591.9 97.1 all-gather.7
  705.4 66.8 reduce-scatter.1
